TPU v7x, 256 devices: a whole 4x4x8 slice. The times are simulated.
256 devices in a mesh: island: 4 (over z_hi, core), tensor: 64 (over y, x, z_lo).
Axes of the slice: x: 4, y: 4, z: 8 (z_hi: 2, z_lo: 4; z = z_hi * 4 + z_lo), core: 2. Of those that a mesh axis runs over, the one named last changes fastest.
Arguments:
- activations: bfloat16 [4, 1024, 5120], P('island', 'tensor'), may hold values from -30 to 30, as said below
- cotangent: bfloat16 [4, 1024, 5120], P('island', 'tensor'), may hold values from -24 to 24
- gate_weight: bfloat16 [4, 6912, 5120], P('island', 'tensor'), may hold values from -6 to 6
- up_weight: bfloat16 [4, 6912, 5120], P('island', 'tensor'), may hold values from -6 to 6
- down_weight: bfloat16 [4, 6912, 5120], P('island', 'tensor'), may hold values from -6 to 6
- gate_control: bfloat16 [4, 6912, 5120], P('island', 'tensor'), may hold values from -4 to 4
- up_control: bfloat16 [4, 6912, 5120], P('island', 'tensor'), may hold values from -4 to 4
- down_control: bfloat16 [4, 6912, 5120], P('island', 'tensor'), may hold values from -4 to 4
Outputs:
- gate_new: bfloat16 [6912, 5120], P('tensor')
- up_new: bfloat16 [6912, 5120], P('tensor')
- down_new: bfloat16 [6912, 5120], P('tensor')
- gate_control_new: bfloat16 [4, 6912, 5120], P('island', 'tensor')
- up_control_new: bfloat16 [4, 6912, 5120], P('island', 'tensor')
- down_control_new: bfloat16 [4, 6912, 5120], P('island', 'tensor')
Inputs may be any that keep to these rules, and one draw needn't show every extreme that they name: `activations`: real values; columns and tokens carry different scales.
All inputs are finite; a program needn't handle non-finite values.
Results may differ from a plain program's by a relative error of at most 0.0095.
Values may be sent and summed in bfloat16 or wider, within the bound.
No kernel may reach another device: no remote copies, remote signals or barrier semaphores. Data moves between devices by JAX's collectives and lax.ppermute only.
A program may use at most 128 MiB of HBM per device.

v0:
```python
import jax
import jax.numpy as jnp
from jax import lax
from jax.sharding import PartitionSpec as P

D = 5120
FF = 6912
EPSILON = 1e-06
STEP_SIZE = 1.0
PROX_PROB = 0.5


def contract_first(left, right):
    return lax.dot_general(
        left, right, (((0,), (0,)), ((), ())), preferred_element_type=jnp.float32
    )


def contract_last(left, right):
    return lax.dot_general(
        left, right, (((1,), (1,)), ((), ())), preferred_element_type=jnp.float32
    )


def normalize(rows):
    wide = rows.astype(jnp.float32)
    mean_square = jnp.mean(wide * wide, axis=-1, keepdims=True)
    return (wide * lax.rsqrt(mean_square + EPSILON)).astype(jnp.bfloat16)


def block_grads(normed, cot_rows, gate_w, up_w, down_w):
    d_scale = D ** (-0.5)
    f_scale = FF ** (-0.5)
    gate_proj = contract_last(normed, gate_w) * d_scale
    up_proj = contract_last(normed, up_w) * d_scale
    sigmoid_gate = jax.nn.sigmoid(gate_proj)
    activated = gate_proj * sigmoid_gate
    hidden = (activated * up_proj).astype(jnp.bfloat16)
    grad_down = contract_first(hidden, cot_rows) * f_scale
    grad_hidden = contract_last(cot_rows, down_w) * f_scale
    grad_gatepre = (
        grad_hidden * up_proj * sigmoid_gate * (1.0 + gate_proj * (1.0 - sigmoid_gate))
    ).astype(jnp.bfloat16)
    grad_uppre = (grad_hidden * activated).astype(jnp.bfloat16)
    grad_gate = contract_first(grad_gatepre, normed) * d_scale
    grad_up = contract_first(grad_uppre, normed) * d_scale
    return (grad_gate, grad_up, grad_down)


def prox_parts(weight, control, grad):
    control_wide = control.astype(jnp.float32)
    local = weight.astype(jnp.float32) - STEP_SIZE * (grad - control_wide)
    return (local, (local - STEP_SIZE / PROX_PROB * control_wide).astype(jnp.bfloat16))


def fresh_control(control, mean_rounded, local):
    wide = control.astype(jnp.float32) + PROX_PROB / STEP_SIZE * (
        mean_rounded.astype(jnp.float32) - local
    )
    return wide.astype(jnp.bfloat16)[None]


def per_device(
    activations,
    cotangent,
    gate_weight,
    up_weight,
    down_weight,
    gate_control,
    up_control,
    down_control,
):
    own_rows = activations[0]
    own_cot = cotangent[0]
    normed = lax.all_gather(normalize(own_rows), "tensor", axis=0, tiled=True)
    whole_cot = lax.all_gather(own_cot, "tensor", axis=0, tiled=True)
    grad_gate, grad_up, grad_down = block_grads(
        normed, whole_cot, gate_weight[0], up_weight[0], down_weight[0]
    )
    local_gate, term_gate = prox_parts(gate_weight[0], gate_control[0], grad_gate)
    local_up, term_up = prox_parts(up_weight[0], up_control[0], grad_up)
    local_down, term_down = prox_parts(down_weight[0], down_control[0], grad_down)
    count = lax.axis_size("island")
    total_gate, total_up, total_down = (
        lax.psum(term_gate, "island").astype(jnp.float32),
        lax.psum(term_up, "island").astype(jnp.float32),
        lax.psum(term_down, "island").astype(jnp.float32),
    )
    mean_gate = (total_gate / count).astype(jnp.bfloat16)
    mean_up = (total_up / count).astype(jnp.bfloat16)
    mean_down = (total_down / count).astype(jnp.bfloat16)
    new_gate_control = fresh_control(gate_control[0], mean_gate, local_gate)
    new_up_control = fresh_control(up_control[0], mean_up, local_up)
    new_down_control = fresh_control(down_control[0], mean_down, local_down)
    return (mean_gate, mean_up, mean_down, new_gate_control, new_up_control, new_down_control)


def solution(mesh):
    placed = (
        P("island", "tensor", None),
        P("island", "tensor", None),
        P("island", "tensor", None),
        P("island", "tensor", None),
        P("island", "tensor", None),
        P("island", "tensor", None),
        P("island", "tensor", None),
        P("island", "tensor", None),
    )
    return jax.shard_map(
        per_device,
        mesh=mesh,
        in_specs=placed,
        out_specs=(
            P("tensor", None),
            P("tensor", None),
            P("tensor", None),
            P("island", "tensor", None),
            P("island", "tensor", None),
            P("island", "tensor", None),
        ),
        check_vma=False,
    )
```

profile of v0, /device:TPU:1, one launch (start us, length us, event | category | flops | bytes accessed | tf_op | source)
XLA Modules:
  0.0 956.3 jit_solution(8239383202195098988)
XLA Ops:
  7.2 0.0 all-gather.4.cloned.1.call-start
  7.2 1.1 fusion.36
  8.3 1.7 fusion.37
  10.0 0.0 all-gather.4.cloned.1.call-update
  10.0 0.0 all-gather.6.cloned.1.call-start
  10.0 0.7 all-gather.6.cloned.1.call-update
  10.8 0.0 copy-start.11
  10.8 0.0 all-reduce.3.cloned.1.call-start
  10.8 343.7 %all-gather.4.cloned.1.call-done = bf16[1024,5120]{1,0:T(8,128)(2,1)} async-done(((bf16[16,5120]{1,0:T(8,128)(2,1)}), bf16[1024,5120]{1,0:T(8,128)(2,1)}) %all-gather.4.cloned.1.call-update) | async-done | bytes 10485776 | tf_op jit(solution)/shard_map/all_gather | solution.py:75
  354.5 7.9 convolution_multiply_fusion.2
  362.4 0.0 copy-start.8
  362.4 3.5 convolution_multiply_fusion.3
  366.0 367.8 %all-gather.6.cloned.1.call-done = bf16[1,1024,5120]{2,1,0:T(8,128)(2,1)} async-done(((bf16[1,16,5120]{2,1,0:T(8,128)(2,1)}), bf16[1,1024,5120]{2,1,0:T(8,128)(2,1)}) %all-gather.6.cloned.1.call-update) | async-done | bytes 10485776 | tf_op jit(solution)/shard_map/all_gather | solution.py:76
  733.8 7.6 fusion.26
  741.4 0.0 copy-start.2
  741.4 7.5 fusion.24
  749.0 0.0 copy-start.4
  749.0 4.4 fusion.18
  753.4 4.5 fusion.21
  757.8 0.0 all-reduce.3.cloned.1.call-update
  757.9 184.1 %all-reduce.3.cloned.1.call-done = (bf16[108,5120]{1,0:T(8,128)(2,1)}, bf16[108,5120]{1,0:T(8,128)(2,1)}, bf16[108,5120]{1,0:T(8,128)(2,1)}) async-done(((bf16[108,5120]{1,0:T(8,128)(2,1)}, bf16[108,5120]{1,0:T(8,128)(2,1)}, bf16[108,5120]{1,0:T(8,128)(2,1)}), (bf16[108,5120]{1,0:T(8,128)(2,1)}, bf16[108,5120]{1,0:T(8,128)(2,1)}, bf16[108,5120]{1,0:T(8,128)(2,1)})) %all-reduce.3.cloned.1.call-update) | async-done | bytes 3317776 | tf_op jit(solution)/shard_map/psum | solution.py:85
  942.0 4.0 fusion.31
  946.0 0.7 copy-done.14
  946.8 3.0 fusion.29
  (33 shorter events, 0.1 us)
Async XLA Ops:
  7.2 347.3 %all-gather.4.cloned.1.call-start = ((), (), s32[]{:S(2)}) async-start(), calls=%async_computation | async-start | bytes 10649600 | tf_op jit(solution)/shard_map/all_gather | solution.py:75
  10.0 723.7 %all-gather.6.cloned.1.call-start = ((), (), s32[]{:S(2)}) async-start(), calls=%async_computation.1 | async-start | bytes 10649600 | tf_op jit(solution)/shard_map/all_gather | solution.py:76
  10.8 351.7 %copy-start.11 = (bf16[1,108,5120]{2,1,0:T(8,128)(2,1)S(1)}, bf16[1,108,5120]{2,1,0:T(8,128)(2,1)}, u32[]{:S(2)}) copy-start(bf16[1,108,5120]{2,1,0:T(8,128)(2,1)} %param.11) | copy-start | bytes 3317764
  10.8 931.2 %all-reduce.3.cloned.1.call-start = ((), (), s32[]{:S(2)}) async-start(), calls=%async_computation.2 | async-start | bytes 6881280 | tf_op jit(solution)/shard_map/psum | solution.py:85
  354.5 7.9 copy-start
  362.4 371.3 %copy-start.8 = (bf16[1,108,5120]{2,1,0:T(8,128)(2,1)S(1)}, bf16[1,108,5120]{2,1,0:T(8,128)(2,1)}, u32[]{:S(2)}) copy-start(bf16[1,108,5120]{2,1,0:T(8,128)(2,1)} %param.12) | copy-start | bytes 3317764
  733.7 7.6 copy-start.6
  733.7 7.7 copy-start.9
  733.7 15.2 %slice-start = ((s8[10485760]{0:T(1024)(128)(4,1)}), s8[4194304]{0:T(1024)(128)(4,1)S(1)}, s32[]{:S(2)}) async-start(s8[10485760]{0:T(1024)(128)(4,1)} %bitcast.56), calls=%async_computation.3 | async-start | bytes 8388608
  733.8 15.2 %slice-start.1 = ((s8[10485760]{0:T(1024)(128)(4,1)}), s8[4194304]{0:T(1024)(128)(4,1)S(1)}, s32[]{:S(2)}) async-start(s8[10485760]{0:T(1024)(128)(4,1)} %bitcast.56), calls=%async_computation.4 | async-start | bytes 8388608
  741.4 7.5 slice-start.2
  741.4 7.5 copy-start.2
  741.4 7.5 copy-start.10
  749.0 4.4 copy-start.4
  749.0 4.4 copy-start.12
  757.8 184.1 %copy-start.3 = (bf16[1,108,5120]{2,1,0:T(8,128)(2,1)S(1)}, bf16[1,108,5120]{2,1,0:T(8,128)(2,1)}, u32[]{:S(2)}) copy-start(bf16[1,108,5120]{2,1,0:T(8,128)(2,1)} %param.13) | copy-start | bytes 3317764
  941.9 4.1 copy-start.1
  941.9 4.1 copy-start.5
  942.0 4.1 copy-start.7
  942.0 4.1 copy-start.13
  942.0 4.8 copy-start.14
Sparse Core Ops, SparseCore 0:
  10.3 344.1 all-gather.3
  356.3 377.4 all-gather.5
  758.0 183.9 all-reduce.2
where the time goes:
time: 956 us
  waiting for transfers between devices  896 us (94%)
  matrix products  35.3 us (4%)
  between operations  13.9 us (1%)
  other arithmetic  9.76 us (1%)
    all_gather x1, waiting for transfers between devices, per_device(): whole_cot = lax.all_gather(own_cot, 'tensor', axis=0, tiled=True)  368 us
    all_gather x1, waiting for transfers between devices, per_device(): normed = lax.all_gather(normalize(own_rows), 'tensor', axis=0, tiled=True)  344 us
    psum x1, waiting for transfers between devices, per_device(): lax.psum(term_gate, 'island').astype(jnp.float32)  184 us
  transfers between devices with their start and end apart: 3, of which 3 were waited for; matrix products, arithmetic and copies ran while one was open for 1% of the time, Pallas kernels for 0%

commit v1 on v0

--- a/solution.py
+++ b/solution.py
@@ -73,7 +73,9 @@
     own_rows = activations[0]
     own_cot = cotangent[0]
     normed = lax.all_gather(normalize(own_rows), "tensor", axis=0, tiled=True)
-    whole_cot = lax.all_gather(own_cot, "tensor", axis=0, tiled=True)
+    whole_cot = jnp.concatenate(
+        lax.all_to_all(jnp.stack([own_cot] * lax.axis_size("tensor")), "tensor", 0, 0), axis=0
+    )
     grad_gate, grad_up, grad_down = block_grads(
         normed, whole_cot, gate_weight[0], up_weight[0], down_weight[0]
     )

time: 956 us -> 698 us (0.73)
  waiting for transfers between devices: 896 us -> 620 us
  starting transfers between devices: 0.12 us -> 13 us
    all_to_all x0 -> x1, waiting for transfers between devices: none -> 409 us  [per_device(): lax.all_to_all(jnp.stack([own_cot] * lax.axis_size('tensor')), 'tensor',...]
    all_gather x1 -> x0, waiting for transfers between devices: 368 us -> none  [per_device(): whole_cot = lax.all_gather(own_cot, 'tensor', axis=0, tiled=True)]
    all_gather x1, waiting for transfers between devices: 344 us -> 45 us  [per_device(): normed = lax.all_gather(normalize(own_rows), 'tensor', axis=0, tiled=True)]
    psum x1, waiting for transfers between devices: 184 us -> 166 us  [per_device(): lax.psum(term_gate, 'island').astype(jnp.float32)]
    all_to_all x0 -> x1, starting transfers between devices: none -> 12.9 us  [per_device(): lax.all_to_all(jnp.stack([own_cot] * lax.axis_size('tensor')), 'tensor',...]
where the time goes in v1:
time: 698 us
  waiting for transfers between devices  620 us (89%)
  matrix products  35.9 us (5%)
  between operations  14.2 us (2%)
  starting transfers between devices  13 us (2%)
  other arithmetic  7.93 us (1%)
    all_to_all x1, waiting for transfers between devices, per_device(): lax.all_to_all(jnp.stack([own_cot] * lax.axis_size('tensor')), 'tensor',...  409 us
    psum x1, waiting for transfers between devices, per_device(): lax.psum(term_gate, 'island').astype(jnp.float32)  166 us
    all_gather x1, waiting for transfers between devices, per_device(): normed = lax.all_gather(normalize(own_rows), 'tensor', axis=0, tiled=True)  45 us
    dot_general x3, matrix products, contract_last(): lax.dot_general(left, right, (((1,), (1,)), ((), ())), preferred_element_...  19.6 us
    dot_general x3, matrix products, contract_first(): lax.dot_general(left, right, (((0,), (0,)), ((), ())), preferred_element_...  16.3 us
  transfers between devices with their start and end apart: 3, of which 3 were waited for; matrix products, arithmetic and copies ran while one was open for 1% of the time, Pallas kernels for 0%

profile of v1, /device:TPU:1, one launch (start us, length us, event | category | flops | bytes accessed | tf_op | source)
XLA Modules:
  0.0 698.0 jit_solution(17461719866586189629)
XLA Ops:
  7.2 6.1 stack.3
  13.3 12.9 %all-to-all-start = ((bf16[64,16,5120]{2,1,0:T(8,128)(2,1)}), bf16[64,16,5120]{2,1,0:T(8,128)(2,1)}, u32[]{:S(2)}, u32[]{:S(2)}) async-start(bf16[64,16,5120]{2,1,0:T(8,128)(2,1)} %stack.3), calls=%async_computation | async-start | bytes 20971520 | tf_op jit(solution)/shard_map/all_to_all | solution.py:77
  26.2 0.0 all-gather.2.cloned.1.call-start
  26.2 0.2 fusion.22
  26.4 0.8 fusion.23
  27.2 0.0 all-gather.2.cloned.1.call-update
  27.2 0.0 all-reduce.3.cloned.1.call-start
  27.2 409.1 %all-to-all-done = bf16[64,16,5120]{2,1,0:T(8,128)(2,1)} async-done(((bf16[64,16,5120]{2,1,0:T(8,128)(2,1)}), bf16[64,16,5120]{2,1,0:T(8,128)(2,1)}, u32[]{:S(2)}, u32[]{:S(2)}) %all-to-all-start) | async-done | bytes 10485792 | tf_op jit(solution)/shard_map/all_to_all | solution.py:77
  436.3 8.4 %convolution_multiply_fusion.5 = f32[1024,108]{0,1:T(8,128)} fusion(bf16[1024,5120]{1,0:T(8,128)(2,1)} %bitcast.2, bf16[1,108,5120]{2,1,0:T(8,128)(2,1)S(1)} %copy-done.8), kind=kOutput, calls=%fused_computation.29 | convolution fusion | flops 1132572672 | bytes 12034048 | tf_op jit(solution)/shard_map/dot_general | solution.py:20
  444.7 45.0 %all-gather.2.cloned.1.call-done = bf16[1024,5120]{1,0:T(8,128)(2,1)} async-done(((bf16[16,5120]{1,0:T(8,128)(2,1)}), bf16[1024,5120]{1,0:T(8,128)(2,1)}) %all-gather.2.cloned.1.call-update) | async-done | bytes 10485776 | tf_op jit(solution)/shard_map/all_gather | solution.py:75
  489.7 7.6 %convolution_multiply_fusion.3 = f32[1024,108]{0,1:T(8,128)S(1)} fusion(bf16[1024,5120]{1,0:T(8,128)(2,1)} %all-gather.2.cloned.1.call-done, bf16[1,108,5120]{2,1,0:T(8,128)(2,1)S(1)} %copy-done.10), kind=kOutput, calls=%fused_computation.27 | convolution fusion | flops 1132572672 | bytes 12034048 | tf_op jit(solution)/shard_map/dot_general | solution.py:20
  497.4 0.0 copy-start.5
  497.4 0.0 copy-start.9
  497.4 3.6 convolution_multiply_fusion.4
  501.0 0.0 copy-start.2
  501.1 7.5 %fusion.13 = (bf16[108,5120]{1,0:T(8,128)(2,1)}, f32[108,5120]{1,0:T(8,128)S(1)}) fusion(bf16[1,108,5120]{2,1,0:T(8,128)(2,1)S(1)} %copy-done.5, bf16[1024,5120]{1,0:T(8,128)(2,1)} %bitcast.2, f32[1024,108]{0,1:T(8,128)S(1)} %convolution_multiply_fusion.4, f32[1024,108]{0,1:T(8,128)S(1)} %convolution_multiply_fusion.3, bf16[1,108,5120]{2,1,0:T(8,128)(2,1)S(1)} %copy-done.9), kind=kOutput, calls=%fused_computation.22 | convolution fusion | flops 1137549312 | bytes 16900096 | tf_op jit(solution)/shard_map/dot_general | solution.py:14
  508.6 0.0 copy-start.3
  508.6 4.3 fusion.7
  513.0 4.4 fusion.10
  517.4 0.0 all-reduce.3.cloned.1.call-update
  517.4 165.9 %all-reduce.3.cloned.1.call-done = (bf16[108,5120]{1,0:T(8,128)(2,1)}, bf16[108,5120]{1,0:T(8,128)(2,1)}, bf16[108,5120]{1,0:T(8,128)(2,1)}) async-done(((bf16[108,5120]{1,0:T(8,128)(2,1)}, bf16[108,5120]{1,0:T(8,128)(2,1)}, bf16[108,5120]{1,0:T(8,128)(2,1)}), (bf16[108,5120]{1,0:T(8,128)(2,1)}, bf16[108,5120]{1,0:T(8,128)(2,1)}, bf16[108,5120]{1,0:T(8,128)(2,1)})) %all-reduce.3.cloned.1.call-update) | async-done | bytes 3317776 | tf_op jit(solution)/shard_map/psum | solution.py:87
  683.4 4.0 fusion.17
  687.4 0.8 copy-done.15
  688.2 3.0 fusion.15
  (30 shorter events, 0.1 us)
Async XLA Ops:
  13.3 13.0 %copy-start.16 = (bf16[1,16,5120]{2,1,0:T(8,128)(2,1)S(1)}, bf16[1,16,5120]{2,1,0:T(8,128)(2,1)}, u32[]{:S(2)}) copy-start(bf16[1,16,5120]{2,1,0:T(8,128)(2,1)} %param.8) | copy-start | bytes 491524
  13.3 423.1 %copy-start.8 = (bf16[1,108,5120]{2,1,0:T(8,128)(2,1)S(1)}, bf16[1,108,5120]{2,1,0:T(8,128)(2,1)}, u32[]{:S(2)}) copy-start(bf16[1,108,5120]{2,1,0:T(8,128)(2,1)} %param.12) | copy-start | bytes 3317764
  13.3 423.1 %all-to-all-start = ((bf16[64,16,5120]{2,1,0:T(8,128)(2,1)}), bf16[64,16,5120]{2,1,0:T(8,128)(2,1)}, u32[]{:S(2)}, u32[]{:S(2)}) async-start(bf16[64,16,5120]{2,1,0:T(8,128)(2,1)} %stack.3), calls=%async_computation | async-start | bytes 20971520 | tf_op jit(solution)/shard_map/all_to_all | solution.py:77
  26.2 463.6 %all-gather.2.cloned.1.call-start = ((), (), s32[]{:S(2)}) async-start(), calls=%async_computation.1 | async-start | bytes 10649600 | tf_op jit(solution)/shard_map/all_gather | solution.py:75
  27.2 656.2 %all-reduce.3.cloned.1.call-start = ((), (), s32[]{:S(2)}) async-start(), calls=%async_computation.2 | async-start | bytes 6881280 | tf_op jit(solution)/shard_map/psum | solution.py:87
  436.3 53.4 %copy-start.10 = (bf16[1,108,5120]{2,1,0:T(8,128)(2,1)S(1)}, bf16[1,108,5120]{2,1,0:T(8,128)(2,1)}, u32[]{:S(2)}) copy-start(bf16[1,108,5120]{2,1,0:T(8,128)(2,1)} %param.10) | copy-start | bytes 3317764
  444.7 52.7 %copy-start.12 = (bf16[1,108,5120]{2,1,0:T(8,128)(2,1)S(1)}, bf16[1,108,5120]{2,1,0:T(8,128)(2,1)}, u32[]{:S(2)}) copy-start(bf16[1,108,5120]{2,1,0:T(8,128)(2,1)} %param.11) | copy-start | bytes 3317764
  489.7 7.6 %copy-start = (bf16[1024,5120]{1,0:T(8,128)(2,1)S(1)}, bf16[1024,5120]{1,0:T(8,128)(2,1)}, u32[]{:S(2)}) copy-start(bf16[1024,5120]{1,0:T(8,128)(2,1)} %all-gather.2.cloned.1.call-done) | copy-start | bytes 31457284
  497.4 3.6 copy-start.5
  497.4 3.6 copy-start.9
  501.0 7.5 %copy-start.2 = (bf16[1,108,5120]{2,1,0:T(8,128)(2,1)S(1)}, bf16[1,108,5120]{2,1,0:T(8,128)(2,1)}, u32[]{:S(2)}) copy-start(bf16[1,108,5120]{2,1,0:T(8,128)(2,1)} %param.13) | copy-start | bytes 3317764
  501.0 7.5 %copy-start.7 = (f32[1024,108]{0,1:T(8,128)S(1)}, f32[1024,108]{0,1:T(8,128)}, u32[]{:S(2)}) copy-start(f32[1024,108]{0,1:T(8,128)} %convolution_multiply_fusion.5) | copy-start | bytes 1327108
  501.1 7.5 %copy-start.11 = (bf16[1,108,5120]{2,1,0:T(8,128)(2,1)S(1)}, bf16[1,108,5120]{2,1,0:T(8,128)(2,1)}, u32[]{:S(2)}) copy-start(bf16[1,108,5120]{2,1,0:T(8,128)(2,1)} %param.10) | copy-start | bytes 3317764
  508.6 4.4 copy-start.3
  508.6 4.4 copy-start.13
  683.4 4.1 copy-start.1
  683.4 4.1 copy-start.4
  683.4 4.1 copy-start.6
  683.4 4.1 copy-start.14
  683.4 4.8 copy-start.15
Sparse Core Ops, SparseCore 0:
  29.3 460.3 all-gather.1
  517.6 165.7 all-reduce.2
